TPU v7x, 256 devices: a whole 4x4x8 slice. The times are simulated.
256 devices in a mesh: dp: 16 (over y_lo, z), lat: 16 (over y_hi, x, core).
Axes of the slice: x: 4, y: 4 (y_hi: 2, y_lo: 2; y = y_hi * 2 + y_lo), z: 8, core: 2. Of those that a mesh axis runs over, the one named last changes fastest.
Arguments:
- tokens: bfloat16 [4096, 8192], P('dp', 'lat'), may hold values from -6 to 6
- enc_weight: bfloat16 [8192, 4096], P(None, 'lat'), may hold values from -0.0625 to 0.0625
- enc_bias: float32 [4096], P('lat'), may hold values from -3 to 3
- dec_weight: bfloat16 [4096, 8192], P('lat'), may hold values from -0.25 to 0.25
- dec_bias: bfloat16 [8192], P('lat'), may hold values from -3 to 3
- block_ids: int32 [16, 8], P('dp'), may hold values from 0 to 31, as said below
- counts: int32 [16], P('dp'), may hold values from 4 to 8
Outputs:
- error: bfloat16 [4096, 8192], P('dp', 'lat')
- grad_enc: float32 [8192, 4096], P('dp', 'lat')
- grad_dec: float32 [4096, 8192], P('lat', 'dp')
Inputs may be any that keep to these rules, and one draw needn't show every extreme that they name: `block_ids`: in each row the 8 entries are different latent block numbers; entries past the row's count are not used.
All inputs are finite; a program needn't handle non-finite values.
Results may differ from a plain program's by a relative error of at most 0.015.
Values may be sent and summed in bfloat16 or wider, within the bound.
No kernel may reach another device: no remote copies, remote signals or barrier semaphores. Data moves between devices by JAX's collectives and lax.ppermute only.
A program may use at most 128 MiB of HBM per device.

v0:
```python
import math

import jax
import jax.numpy as jnp
from jax import lax
from jax.sharding import PartitionSpec as P

BLK = 128


def block_flags(block_ids, counts, owned_id, token_total):
    slot_index = lax.broadcasted_iota(jnp.int32, block_ids.shape, 1)
    is_live = slot_index < counts[:, None]
    hit_count = jnp.sum(jnp.where(is_live & (block_ids == owned_id), 1, 0), axis=1)
    block_live = (hit_count > 0).astype(jnp.float32)
    row_mask = jnp.repeat(block_live, token_total // block_ids.shape[0])[:, None]
    return (jnp.sum(hit_count) > 0, row_mask)


def encode_block(full_tokens, weight_cols, bias_cols, weight_rows, row_mask, is_active):

    def encode_active_path(unused_arg):
        preact = jnp.dot(full_tokens, weight_cols, preferred_element_type=jnp.float32) + bias_cols
        activations = (jnp.maximum(preact, 0.0) * row_mask).astype(jnp.bfloat16)
        return (activations, jnp.dot(activations, weight_rows, preferred_element_type=jnp.float32))

    def encode_quiet_path(unused_arg):
        return (
            jnp.zeros((full_tokens.shape[0], weight_cols.shape[1]), jnp.bfloat16),
            jnp.zeros((full_tokens.shape[0], weight_rows.shape[1]), jnp.float32),
        )

    return lax.cond(is_active, encode_active_path, encode_quiet_path, 0)


def fold_block(fold_state, err_piece, weight_rows, act_block, is_active):

    def fold_active_path(current):
        pre_part = lax.dot_general(
            err_piece, weight_rows, (((1,), (1,)), ((), ())), preferred_element_type=jnp.float32
        )
        product = lax.dot_general(
            act_block, err_piece, (((0,), (0,)), ((), ())), preferred_element_type=jnp.float32
        )
        return (pre_part, product)

    def fold_quiet_path(current):
        return current

    return lax.cond(is_active, fold_active_path, fold_quiet_path, fold_state)


def enc_grad_block(full_tokens, gated, is_active):

    def enc_active_path(unused_arg):
        return lax.dot_general(
            full_tokens, gated, (((0,), (0,)), ((), ())), preferred_element_type=jnp.float32
        )

    def enc_quiet_path(unused_arg):
        return jnp.zeros((full_tokens.shape[1], gated.shape[1]), jnp.float32)

    return lax.cond(is_active, enc_active_path, enc_quiet_path, 0)


def local(tokens, enc_weight, enc_bias, dec_weight, dec_bias, block_ids, counts):
    full_tokens, full_bias = (
        lax.all_gather(tokens, "lat", axis=1, tiled=True),
        lax.all_gather(dec_bias, "lat", axis=0, tiled=True),
    )
    token_total = full_tokens.shape[0]
    feature_count = full_tokens.shape[1]
    owned_count = enc_weight.shape[1] // BLK
    first_block = lax.axis_index("lat") * owned_count
    flag_list = []
    mask_list = []
    act_list = []
    partial_value = jnp.zeros((token_total, feature_count), jnp.float32)
    for local_block in range(owned_count):
        col_start = local_block * BLK
        is_active, row_mask = block_flags(block_ids, counts, first_block + local_block, token_total)
        flag_list.append(is_active)
        mask_list.append(row_mask)
        activations, contrib = encode_block(
            full_tokens,
            enc_weight[:, col_start : col_start + BLK],
            enc_bias[col_start : col_start + BLK],
            dec_weight[col_start : col_start + BLK],
            row_mask,
            is_active,
        )
        act_list.append(activations)
        partial_value = partial_value + contrib

    def fold_all(carry, err_piece):
        block_states, assembled = carry
        new_states = tuple(
            (
                fold_block(
                    block_states[local_block],
                    err_piece,
                    dec_weight[local_block * BLK : (local_block + 1) * BLK],
                    act_list[local_block],
                    flag_list[local_block],
                )
                for local_block in range(owned_count)
            )
        )
        assembled = err_piece
        return (new_states, assembled)

    start_blocks = tuple(
        (
            (
                jnp.zeros((token_total, BLK), jnp.float32),
                jnp.zeros((BLK, feature_count), jnp.float32),
            )
            for local_block in range(owned_count)
        )
    )
    start_state = (start_blocks, jnp.zeros((token_total, feature_count), jnp.bfloat16))
    share_sum = lax.psum_scatter(
        partial_value.astype(jnp.bfloat16), "lat", scatter_dimension=1, tiled=True
    ).astype(jnp.float32)
    err_share = (
        share_sum + dec_bias.astype(jnp.float32)[None, :] - tokens.astype(jnp.float32)
    ).astype(jnp.bfloat16)
    folded, err_full = fold_all(start_state, lax.all_gather(err_share, "lat", axis=1, tiled=True))
    gated_list = []
    dec_blocks = []
    for local_block in range(owned_count):
        pre_part, grad_part = folded[local_block]
        gated_list.append(jnp.where(act_list[local_block] > 0, pre_part, 0.0).astype(jnp.bfloat16))
        dec_blocks.append(grad_part)
    scale_factor = 1.0 / math.sqrt(token_total * lax.axis_size("dp"))
    enc_blocks = []
    for local_block in range(owned_count):
        enc_blocks.append(
            enc_grad_block(full_tokens, gated_list[local_block], flag_list[local_block])
        )
    enc_grad = jnp.concatenate(enc_blocks, axis=1)
    dec_grad = jnp.concatenate(dec_blocks, axis=0)
    enc_sum, dec_sum = (
        lax.psum_scatter(
            enc_grad.astype(jnp.bfloat16), "dp", scatter_dimension=0, tiled=True
        ).astype(jnp.float32),
        lax.psum_scatter(
            dec_grad.astype(jnp.bfloat16), "dp", scatter_dimension=1, tiled=True
        ).astype(jnp.float32),
    )
    return (err_share, enc_sum * scale_factor, dec_sum * scale_factor)


def solution(mesh):
    placed = (
        P("dp", "lat"),
        P(None, "lat"),
        P("lat"),
        P("lat", None),
        P("lat"),
        P("dp", None),
        P("dp"),
    )
    return jax.shard_map(
        local,
        mesh=mesh,
        in_specs=placed,
        out_specs=(P("dp", "lat"), P("dp", "lat"), P("lat", "dp")),
        check_vma=False,
    )
```

profile of v0, /device:TPU:6, one launch (start us, length us, event | category | flops | bytes accessed | tf_op | source)
XLA Modules:
  0.0 441.8 jit_solution(9756478937163688735)
XLA Ops:
  7.2 0.0 all-gather.3.cloned.1.call-start
  7.2 0.7 all-gather.3.cloned.1.call-update
  7.9 0.0 reduce-scatter.4.cloned.1.call-start
  8.6 1.3 fusion.29
  11.2 0.0 copy-start.8
  11.2 4.0 fusion.30
  15.2 61.4 %all-gather.3.cloned.1.call-done = bf16[256,8192]{1,0:T(8,128)(2,1)} async-done(((bf16[256,512]{1,0:T(8,128)(2,1)}), bf16[256,8192]{1,0:T(8,128)(2,1)}) %all-gather.3.cloned.1.call-update) | async-done | bytes 4194320 | tf_op jit(solution)/shard_map/all_gather | solution.py:68
  76.6 0.0 copy-done.8
  76.6 1.6 conditional.7
  76.6 0.9 broadcast.54
  77.6 0.6 broadcast.53
  78.2 0.0 copy-start.2
  78.2 3.3 copy-done.2
  81.5 4.8 %conditional.6 = (bf16[256,128]{1,0:T(8,128)(2,1)}, f32[256,8192]{1,0:T(8,128)}) conditional(s32[]{:T(128)} %convert_element_type.61, () %tuple.52, (bf16[8192,256]{1,0:T(8,128)(2,1)}, bf16[256,8192]{1,0:T(8,128)(2,1)}, f32[256]{0:T(256)S(1)}, pred[]{:T(512)}, bf16[128,8192]{1,0:T(8,128)(2,1)}) %tuple.94), branch_computations={%region_1.2_spmd, %region_2.3_spmd} | conditional | flops 1073872896 | bytes 25298484 | solution.py:33
  81.5 4.2 broadcast.51
  85.7 0.6 broadcast.50
  86.3 8.8 %add_convert_fusion = bf16[256,8192]{1,0:T(8,128)(2,1)} fusion(f32[256,8192]{1,0:T(8,128)} %get-tuple-element.85, f32[256,8192]{1,0:T(8,128)} %copy-done.2), kind=kLoop, calls=%fused_computation.14 | loop fusion | flops 4194304 | bytes 20971520 | tf_op jit(solution)/shard_map/convert_element_type | solution.py:123
  95.1 0.0 copy-start.7
  95.1 0.0 reduce-scatter.4.cloned.1.call-update
  95.1 0.0 all-gather.5.cloned.1.call-start
  95.2 0.6 copy-done.7
  95.8 95.6 %reduce-scatter.4.cloned.1.call-done = bf16[256,512]{1,0:T(8,128)(2,1)} async-done(((bf16[256,8192]{1,0:T(8,128)(2,1)}), bf16[256,512]{1,0:T(8,128)(2,1)}) %reduce-scatter.4.cloned.1.call-update) | async-done | bytes 262160 | tf_op jit(solution)/shard_map/reduce_scatter | solution.py:122
  191.4 0.0 copy-done.6
  191.4 1.7 subtract_convert_fusion
  193.1 0.0 all-gather.5.cloned.1.call-update
  193.2 0.0 reduce-scatter.8.cloned.1.call-start
  193.2 63.9 %all-gather.5.cloned.1.call-done = bf16[256,8192]{1,0:T(8,128)(2,1)} async-done(((bf16[256,512]{1,0:T(8,128)(2,1)}), bf16[256,8192]{1,0:T(8,128)(2,1)}) %all-gather.5.cloned.1.call-update) | async-done | bytes 4194320 | tf_op jit(solution)/shard_map/all_gather | solution.py:128
  257.1 0.2 conditional.8
  257.1 0.2 broadcast.65
  257.3 0.0 copy-start.5
  257.3 1.3 copy-done.5
  258.6 1.8 conditional.10
  258.6 1.6 broadcast.67
  260.4 4.6 %pad_maximum_fusion.1 = bf16[256,8192]{1,0:T(8,128)(2,1)} fusion(bf16[128,8192]{1,0:T(8,128)(2,1)} %get-tuple-element.98, bf16[128,8192]{1,0:T(8,128)(2,1)} %copy-done.5), kind=kLoop, calls=%fused_computation.16 | loop fusion | flops 8388608 | bytes 8388608 | tf_op jit(solution)/shard_map/concatenate | solution.py:142
  265.0 0.0 reduce-scatter.8.cloned.1.call-update
  265.0 0.0 reduce-scatter.6.cloned.1.call-start
  265.1 0.9 select_convert_fusion.1
  266.0 0.3 conditional.9
  266.0 0.3 broadcast.58
  266.3 0.9 select_convert_fusion
  267.1 1.7 conditional.11
  267.1 1.7 broadcast.61
  268.8 4.0 pad_maximum_fusion
  272.9 0.0 reduce-scatter.6.cloned.1.call-update
  272.9 81.1 %reduce-scatter.8.cloned.1.call-done = bf16[256,512]{1,0:T(8,128)(2,1)} async-done(((bf16[256,8192]{1,0:T(8,128)(2,1)}), bf16[256,512]{1,0:T(8,128)(2,1)}) %reduce-scatter.8.cloned.1.call-update) | async-done | bytes 262160 | tf_op jit(solution)/shard_map/reduce_scatter | solution.py:147
  354.0 1.8 convert_multiply_fusion
  355.8 77.7 %reduce-scatter.6.cloned.1.call-done = bf16[512,256]{1,0:T(8,128)(2,1)} async-done(((bf16[8192,256]{1,0:T(8,128)(2,1)}), bf16[512,256]{1,0:T(8,128)(2,1)}) %reduce-scatter.6.cloned.1.call-update) | async-done | bytes 262160 | tf_op jit(solution)/shard_map/reduce_scatter | solution.py:144
  433.5 1.8 convert_multiply_fusion.1
  (4 shorter events, 0.0 us)
Async XLA Ops:
  7.2 69.5 %all-gather.3.cloned.1.call-start = ((), (), s32[]{:S(2)}) async-start(), calls=%async_computation.3 | async-start | bytes 4456448 | tf_op jit(solution)/shard_map/all_gather | solution.py:68
  7.9 183.5 %reduce-scatter.4.cloned.1.call-start = ((), (), s32[]{:S(2)}) async-start(), calls=%async_computation.4 | async-start | bytes 4456448 | tf_op jit(solution)/shard_map/reduce_scatter | solution.py:122
  11.2 65.4 %copy-start.8 = (f32[256]{0:T(256)S(1)}, f32[256]{0:T(256)}, u32[]{:S(2)}) copy-start(f32[256]{0:T(256)} %param.21) | copy-start | bytes 3076
  78.2 3.3 copy-start.2
  95.1 0.7 copy-start.7
  95.1 96.3 %copy-start.6 = (bf16[256,512]{1,0:T(8,128)(2,1)S(1)}, bf16[256,512]{1,0:T(8,128)(2,1)}, u32[]{:S(2)}) copy-start(bf16[256,512]{1,0:T(8,128)(2,1)} %param.19) | copy-start | bytes 786436
  95.1 162.0 %all-gather.5.cloned.1.call-start = ((), (), s32[]{:S(2)}) async-start(), calls=%async_computation.5 | async-start | bytes 4456448 | tf_op jit(solution)/shard_map/all_gather | solution.py:128
  193.2 160.9 %reduce-scatter.8.cloned.1.call-start = ((), (), s32[]{:S(2)}) async-start(), calls=%async_computation.7 | async-start | bytes 4456448 | tf_op jit(solution)/shard_map/reduce_scatter | solution.py:147
  257.3 1.3 copy-start.5
  265.0 168.4 %reduce-scatter.6.cloned.1.call-start = ((), (), s32[]{:S(2)}) async-start(), calls=%async_computation.6 | async-start | bytes 4456448 | tf_op jit(solution)/shard_map/reduce_scatter | solution.py:144
Sparse Core Ops, SparseCore 0:
  10.5 66.0 all-gather.2
  95.2 96.1 reduce-scatter.3
  194.5 62.4 all-gather.4
  265.2 88.8 reduce-scatter.7
  356.4 77.0 reduce-scatter.5
where the time goes:
time: 442 us
  waiting for transfers between devices  380 us (86%)
  other arithmetic  25.8 us (6%)
  local copies, waits for them, and re-layouts  19.3 us (4%)
  between operations  15.8 us (4%)
    reduce_scatter x1, waiting for transfers between devices, local(): lax.psum_scatter(partial_value.astype(jnp.bfloat16), 'lat', scatter_dimen...  95.6 us
    reduce_scatter x1, waiting for transfers between devices, local(): lax.psum_scatter(dec_grad.astype(jnp.bfloat16), 'dp', scatter_dimension=1...  81.1 us
    reduce_scatter x1, waiting for transfers between devices, local(): lax.psum_scatter(enc_grad.astype(jnp.bfloat16), 'dp', scatter_dimension=0...  77.7 us
    all_gather x1, waiting for transfers between devices, local(): lax.all_gather(err_share, 'lat', axis=1, tiled=True)  63.9 us
    all_gather x1, waiting for transfers between devices, local(): lax.all_gather(tokens, 'lat', axis=1, tiled=True)  61.4 us
    another operation x10, local copies, waits for them, and re-layouts  10.1 us
  transfers between devices with their start and end apart: 5, of which 5 were waited for; matrix products, arithmetic and copies ran while one was open for 3% of the time, Pallas kernels for 0%

commit v1 on v0

v1 whole, which is shorter than its diff:
```python
import math

import jax
import jax.numpy as jnp
from jax import lax
from jax.experimental import pallas as pl
from jax.experimental.pallas import tpu as pltpu
from jax.sharding import PartitionSpec as P

BLK = 128
F32 = jnp.float32
BF16 = jnp.bfloat16


def exchange(x, axis):
    return lax.all_to_all(x, axis, 0, 0, tiled=False)


def split3(x):
    hi = lax.reduce_precision(x, 8, 7)
    rest = x - hi
    mid = lax.reduce_precision(rest, 8, 7)
    return hi, mid, rest - mid


def pick_body(ids_ref, table_ref, out_ref):
    groups, rows, _ = out_ref.shape
    slots = ids_ref.shape[1]
    sub = rows // (2 * slots)

    def step(t, carry):
        for k in range(slots):
            block = ids_ref[t, k]
            for w in range(2):
                src = pl.multiple_of((w * 2 + block % 2) * sub, sub)
                out_ref[t, pl.ds((w * slots + k) * sub, sub), :] = table_ref[block // 2, pl.ds(src, sub), :]
        return carry

    lax.fori_loop(0, groups, step, 0)


def pick(ids, table, sub):
    groups, slots = ids.shape
    return pl.pallas_call(
        pick_body,
        out_shape=jax.ShapeDtypeStruct((groups, 2 * slots * sub, BLK), BF16),
        in_specs=[pl.BlockSpec(memory_space=pltpu.SMEM), pl.BlockSpec(memory_space=pltpu.VMEM)],
        out_specs=pl.BlockSpec(memory_space=pltpu.VMEM),
        name="pick",
    )(ids, table)


def gather_sum_body(ids_ref, parts_ref, out_ref, acc_ref):
    groups, rows, _ = parts_ref.shape
    slots = ids_ref.shape[1]
    sub = rows // (2 * slots)
    acc_ref[...] = jnp.zeros_like(acc_ref)

    def step(t, carry):
        for k in range(slots):
            block = ids_ref[t, k]
            for w in range(2):
                part = parts_ref[t, pl.ds((w * slots + k) * sub, sub), :].astype(F32)
                acc_ref[block, pl.ds(w * sub, sub), :] += part
        return carry

    lax.fori_loop(0, groups, step, 0)
    out_ref[...] = acc_ref[...].astype(BF16)


def gather_sum(ids, parts, blocks):
    slots = ids.shape[1]
    sub = parts.shape[1] // (2 * slots)
    return pl.pallas_call(
        gather_sum_body,
        out_shape=jax.ShapeDtypeStruct((blocks, 2 * sub, BLK), BF16),
        in_specs=[pl.BlockSpec(memory_space=pltpu.SMEM), pl.BlockSpec(memory_space=pltpu.VMEM)],
        out_specs=pl.BlockSpec(memory_space=pltpu.VMEM),
        scratch_shapes=[pltpu.VMEM((blocks, 2 * sub, BLK), F32)],
        name="gather_sum",
    )(ids, parts)


def local(tokens, enc_weight, enc_bias, dec_weight, dec_bias, block_ids, counts):
    n_dp, n_lat = lax.axis_size("dp"), lax.axis_size("lat")
    d, t = lax.axis_index("dp"), lax.axis_index("lat")
    token_count, width = tokens.shape
    owned = enc_weight.shape[1] // BLK
    blocks = owned * n_lat
    slots = block_ids.shape[1]
    sub = width // n_lat
    flip = [(i * n_lat + j, j * n_dp + i) for i in range(n_dp) for j in range(n_lat)]

    bias_rows = jnp.broadcast_to(dec_bias[None, :], (16, width))
    moved = lax.ppermute(jnp.concatenate([tokens, bias_rows], axis=0), ("dp", "lat"), flip)
    tok, out_bias = moved[:token_count], moved[token_count : token_count + 1]

    listed = jnp.concatenate([block_ids, counts[:, None]], axis=1)
    listed = jnp.pad(listed, ((0, 0), (0, BLK - slots - 1)))
    lists = exchange(jnp.broadcast_to(listed[None], (n_dp, 1, BLK)), "dp")[:, 0, :]
    ids = jnp.clip(lists[:, :slots], 0, blocks - 1)
    my_list = lax.dynamic_slice_in_dim(lists, t, 1, 0)
    my_ids = jnp.clip(my_list[0, :slots], 0, blocks - 1)
    live = jnp.arange(slots) < my_list[0, slots]
    live_row = jnp.repeat(live, BLK)[None, :]

    enc_part = lax.dynamic_slice_in_dim(enc_weight, d * width, width, 0)
    dec_part = lax.dynamic_slice_in_dim(dec_weight, d * width, width, 1).T
    spread = jnp.stack([enc_part, dec_part]).reshape(2, n_lat, sub, owned, BLK)
    spread = spread.transpose(1, 0, 3, 2, 4).reshape(n_lat, 2 * owned * sub, BLK)
    bias_parts = jnp.stack(split3(enc_bias.reshape(owned, BLK))).reshape(3 * owned, BLK)
    bias_parts = jnp.pad(bias_parts, ((0, 8 - 3 * owned), (0, 0))).astype(BF16)
    spread = jnp.concatenate([spread, jnp.broadcast_to(bias_parts[None], (n_lat, 8, BLK))], axis=1)
    table = exchange(spread, "lat")
    all_bias = table[:, 2 * owned * sub :, :].astype(F32)
    all_bias = all_bias[:, :owned] + all_bias[:, owned : 2 * owned] + all_bias[:, 2 * owned : 3 * owned]
    my_bias = all_bias.reshape(blocks, BLK)[my_ids].reshape(1, slots * BLK)
    picked = exchange(pick(ids, table, sub), "lat")
    picked = picked.reshape(n_lat, 2, slots, sub, BLK).transpose(1, 0, 3, 2, 4)
    picked = picked.reshape(2, width, slots * BLK)
    enc_sel, dec_sel = picked[0], picked[1]

    share = token_count // n_dp
    partial = jnp.dot(tok, enc_sel, preferred_element_type=F32)
    preact = jnp.sum(exchange(partial.reshape(n_dp, share, slots * BLK), "dp"), axis=0) + my_bias
    act_share = jnp.where(live_row, jnp.maximum(preact, 0.0), 0.0)
    gate = act_share > 0
    act_share = act_share.astype(BF16)
    acts = exchange(jnp.broadcast_to(act_share[None], (n_dp, share, slots * BLK)), "dp")
    acts = acts.reshape(token_count, slots * BLK)

    recon = lax.dot_general(acts, dec_sel, (((1,), (1,)), ((), ())), preferred_element_type=F32)
    error = (recon + out_bias.astype(F32) - tok.astype(F32)).astype(BF16)
    error_out = lax.ppermute(error, ("dp", "lat"), [(b, a) for a, b in flip])

    back = jnp.dot(error, dec_sel, preferred_element_type=F32).astype(BF16)
    back = jnp.sum(exchange(back.reshape(n_dp, share, slots * BLK), "dp").astype(F32), axis=0)
    back = jnp.where(gate, back, 0.0).astype(BF16)
    gated = exchange(jnp.broadcast_to(back[None], (n_dp, share, slots * BLK)), "dp")
    gated = gated.reshape(token_count, slots * BLK)

    over_tokens = (((0,), (0,)), ((), ()))
    dec_grad = lax.dot_general(error, acts, over_tokens, preferred_element_type=F32).astype(BF16)
    enc_grad = lax.dot_general(tok, gated, over_tokens, preferred_element_type=F32).astype(BF16)
    grads = jnp.stack([enc_grad, dec_grad]).reshape(2, n_lat, sub, slots, BLK)
    grads = grads.transpose(1, 0, 3, 2, 4).reshape(n_lat, 2 * slots * sub, BLK)
    summed = gather_sum(ids, exchange(grads, "lat"), blocks)
    done = exchange(summed.reshape(n_lat, owned * 2 * sub, BLK), "lat")
    done = done.reshape(n_lat, owned, 2, sub, BLK).astype(F32) * (1.0 / math.sqrt(token_count * n_dp))
    enc_out = done[:, :, 0].transpose(0, 2, 1, 3).reshape(width, owned * BLK)
    dec_out = done[:, :, 1].transpose(1, 3, 0, 2).reshape(owned * BLK, width)
    return error_out, enc_out, dec_out


def solution(mesh):
    placed = (
        P("dp", "lat"),
        P(None, "lat"),
        P("lat"),
        P("lat", None),
        P("lat"),
        P("dp", None),
        P("dp"),
    )
    return jax.shard_map(
        local,
        mesh=mesh,
        in_specs=placed,
        out_specs=(P("dp", "lat"), P("dp", "lat"), P("lat", "dp")),
        check_vma=False,
    )
```

time: 442 us -> 258 us (0.58); the launches traced: 442 us -> 253 us
  waiting for transfers between devices: 380 us -> 115 us
  starting transfers between devices: 0.2 us -> 54.6 us
  blocking collectives: 0 us -> 53.8 us
  other arithmetic: 25.8 us -> 4.88 us
  between operations: 15.8 us -> 1.66 us
  Pallas kernels: 0 us -> 6.66 us
  local copies, waits for them, and re-layouts: 19.3 us -> 13.3 us
    reduce_scatter x3 -> x0, waiting for transfers between devices: 254 us -> none  [the longest x1 95.6 us: local(): lax.psum_scatter(partial_value.astype(jnp.bfloat16), 'lat', scatter_dimen...]
    all_gather x2 -> x0, waiting for transfers between devices: 125 us -> none  [the longest x1 63.9 us: local(): lax.all_gather(err_share, 'lat', axis=1, tiled=True)]
    all_to_all x0 -> x7, waiting for transfers between devices: none -> 78.1 us  [exchange(): return lax.all_to_all(x, axis, 0, 0, tiled=False)]
    all_to_all x0 -> x2, blocking collectives: none -> 53.8 us  [exchange(): return lax.all_to_all(x, axis, 0, 0, tiled=False)]
    all_to_all x0 -> x7, starting transfers between devices: none -> 48.2 us  [exchange(): return lax.all_to_all(x, axis, 0, 0, tiled=False)]
    ppermute x0 -> x2, waiting for transfers between devices: none -> 36.9 us  [the longest x1 19.3 us: local(): lax.ppermute(jnp.concatenate([tokens, bias_rows], axis=0), ('dp', 'lat'),...]
    convert_element_type x5 -> x3, other arithmetic: 12.2 us -> 0.8 us  [the longest x1 0.76 us: local(): all_bias = table[:, 2 * owned * sub:, :].astype(F32)]
    another operation x10 -> x4, local copies, waits for them, and re-layouts: 10.1 us -> 0.64 us  [the longest x2 0.5 us: local(): grads = jnp.stack([enc_grad, dec_grad]).reshape(2, n_lat, sub, slots, BLK)]
  transfers between devices with their start and end apart: 5 -> 9, of which waited for: 5 -> 8; matrix products, arithmetic and copies ran while one was open for 3% -> 3% of each run, Pallas kernels for 0% -> 0%
where the time goes in v1:
time: 258 us; the launch traced here: 253 us
  waiting for transfers between devices  115 us (45%)
  starting transfers between devices  54.6 us (21%)
  blocking collectives  53.8 us (21%)
  local copies, waits for them, and re-layouts  13.3 us (5%)
  Pallas kernels  6.66 us (3%)
  other arithmetic  4.88 us (2%)
  matrix products  3.25 us (1%)
    all_to_all x7, waiting for transfers between devices, exchange(): return lax.all_to_all(x, axis, 0, 0, tiled=False)  78.1 us
    all_to_all x2, blocking collectives, exchange(): return lax.all_to_all(x, axis, 0, 0, tiled=False)  53.8 us
    all_to_all x7, starting transfers between devices, exchange(): return lax.all_to_all(x, axis, 0, 0, tiled=False)  48.2 us
    ppermute x1, waiting for transfers between devices, local(): lax.ppermute(jnp.concatenate([tokens, bias_rows], axis=0), ('dp', 'lat'),...  19.3 us
    ppermute x1, waiting for transfers between devices, local(): error_out = lax.ppermute(error, ('dp', 'lat'), [(b, a) for a, b in flip])  17.6 us
  transfers between devices with their start and end apart: 9, of which 8 were waited for; matrix products, arithmetic and copies ran while one was open for 3% of the time, Pallas kernels for 0%

profile of v1, /device:TPU:6, one launch (start us, length us, event | category | flops | bytes accessed | tf_op | source)
XLA Modules:
  0.0 253.2 jit_solution(12069652981029642680)
XLA Ops:
  1.3 0.7 pad_add_fusion
  2.0 0.6 broadcast_in_dim.32
  2.6 9.6 %all-to-all-start = ((s32[16,1,128]{2,1,0:T(1,128)}), s32[16,1,128]{2,1,0:T(1,128)S(1)}, u32[]{:S(2)}, u32[]{:S(2)}) async-start(s32[16,1,128]{2,1,0:T(1,128)} %broadcast_in_dim.32), calls=%async_computation | async-start | bytes 16384 | tf_op jit(solution)/shard_map/all_to_all | solution.py:16
  12.2 1.0 dynamic-slice_bitcast_fusion
  13.4 1.0 constant_dynamic-slice_fusion
  14.5 0.7 maximum_bitcast_fusion
  15.4 0.9 pad_maximum_fusion.1
  16.3 4.3 %all-to-all-done = s32[16,1,128]{2,1,0:T(1,128)S(1)} async-done(((s32[16,1,128]{2,1,0:T(1,128)}), s32[16,1,128]{2,1,0:T(1,128)S(1)}, u32[]{:S(2)}, u32[]{:S(2)}) %all-to-all-start) | async-done | bytes 8224 | tf_op jit(solution)/shard_map/all_to_all | solution.py:16
  20.6 7.1 %all-to-all-start.1 = ((bf16[16,136,128]{2,1,0:T(8,128)(2,1)}), bf16[16,136,128]{2,1,0:T(8,128)(2,1)S(1)}, u32[]{:S(2)}, u32[]{:S(2)}) async-start(bf16[16,136,128]{2,1,0:T(8,128)(2,1)} %pad_maximum_fusion.1), calls=%async_computation.1 | async-start | bytes 1114112 | tf_op jit(solution)/shard_map/all_to_all | solution.py:16
  27.7 0.6 slice_clamp_fusion.ids_ref
  28.4 9.2 %all-to-all-done.1.table_ref = bf16[16,136,128]{2,1,0:T(8,128)(2,1)S(1)} async-done(((bf16[16,136,128]{2,1,0:T(8,128)(2,1)}), bf16[16,136,128]{2,1,0:T(8,128)(2,1)S(1)}, u32[]{:S(2)}, u32[]{:S(2)}) %all-to-all-start.1) | async-done | bytes 557088 | tf_op jit(solution)/shard_map/all_to_all | solution.py:16
  37.5 0.8 copy-done
  38.3 3.5 %pick.1 = bf16[16,512,128]{2,1,0:T(8,128)(2,1)} custom-call(s32[16,8]{1,0:T(8,128)} %slice_clamp_fusion.ids_ref, bf16[16,136,128]{2,1,0:T(8,128)(2,1)} %copy-done), custom_call_target="tpu_custom_call" | custom-call | tf_op jit(solution)/shard_map/pick/pallas_call | solution.py:44
  41.8 6.7 %all-to-all-start.2 = ((bf16[16,512,128]{2,1,0:T(8,128)(2,1)}), bf16[16,512,128]{2,1,0:T(8,128)(2,1)S(1)}, u32[]{:S(2)}, u32[]{:S(2)}) async-start(bf16[16,512,128]{2,1,0:T(8,128)(2,1)} %pick.1), calls=%async_computation.2 | async-start | bytes 4194304 | tf_op jit(solution)/shard_map/all_to_all | solution.py:16
  48.6 2.2 collective-permute-start
  50.8 19.3 %collective-permute-done = bf16[272,512]{1,0:T(8,128)(2,1)S(1)} collective-permute-done((bf16[272,512]{1,0:T(8,128)(2,1)S(1)}, bf16[272,512]{1,0:T(8,128)(2,1)S(1)}, u32[]{:S(2)}, u32[]{:S(2)}) %collective-permute-start) | collective-permute-done | bytes 278560 | tf_op jit(solution)/shard_map/ppermute | solution.py:95
  70.1 10.5 %all-to-all-done.2 = bf16[16,512,128]{2,1,0:T(8,128)(2,1)S(1)} async-done(((bf16[16,512,128]{2,1,0:T(8,128)(2,1)}), bf16[16,512,128]{2,1,0:T(8,128)(2,1)S(1)}, u32[]{:S(2)}, u32[]{:S(2)}) %all-to-all-start.2) | async-done | bytes 2097184 | tf_op jit(solution)/shard_map/all_to_all | solution.py:16
  80.6 1.0 copy.63
  81.7 0.5 reshape.233
  82.2 0.4 slice-done
  82.7 1.4 fusion.13
  84.1 9.3 %all-to-all-start.3 = ((f32[16,16,1024]{2,1,0:T(8,128)}), f32[16,16,1024]{2,1,0:T(8,128)S(1)}, u32[]{:S(2)}, u32[]{:S(2)}) async-start(f32[16,16,1024]{2,1,0:T(8,128)} %fusion.13), calls=%async_computation.3 | async-start | bytes 2097152 | tf_op jit(solution)/shard_map/all_to_all | solution.py:16
  93.4 0.6 slice.41
  94.0 0.6 iota_compare_fusion
  94.7 0.8 slice_convert_fusion
  95.5 0.6 gather_fusion
  96.1 24.6 %all-to-all-done.3 = f32[16,16,1024]{2,1,0:T(8,128)S(1)} async-done(((f32[16,16,1024]{2,1,0:T(8,128)}), f32[16,16,1024]{2,1,0:T(8,128)S(1)}, u32[]{:S(2)}, u32[]{:S(2)}) %all-to-all-start.3) | async-done | bytes 1048608 | tf_op jit(solution)/shard_map/all_to_all | solution.py:16
  120.8 0.9 broadcast_in_dim.61
  121.6 4.4 %all-to-all-start.4 = ((bf16[16,16,1024]{2,1,0:T(8,128)(2,1)}), bf16[16,16,1024]{2,1,0:T(8,128)(2,1)S(1)}, u32[]{:S(2)}, u32[]{:S(2)}) async-start(bf16[16,16,1024]{2,1,0:T(8,128)(2,1)} %broadcast_in_dim.61), calls=%async_computation.4 | async-start | bytes 1048576 | tf_op jit(solution)/shard_map/all_to_all | solution.py:16
  126.0 15.6 %all-to-all-done.4 = bf16[16,16,1024]{2,1,0:T(8,128)(2,1)S(1)} async-done(((bf16[16,16,1024]{2,1,0:T(8,128)(2,1)}), bf16[16,16,1024]{2,1,0:T(8,128)(2,1)S(1)}, u32[]{:S(2)}, u32[]{:S(2)}) %all-to-all-start.4) | async-done | bytes 524320 | tf_op jit(solution)/shard_map/all_to_all | solution.py:16
  141.6 0.5 subtract_convert_fusion
  142.1 0.4 convolution_convert_fusion.2
  142.5 19.7 %all_to_all.45 = bf16[16,16,1024]{2,1,0:T(8,128)(2,1)S(1)} all-to-all(bf16[16,16,1024]{2,1,0:T(8,128)(2,1)S(1)} %bitcast.106), channel_id=1, replica_groups=mesh['dp'=16,'lat'=16] {'dp'}, dimensions={0} | all-to-all | bytes 1048576 | tf_op jit(solution)/shard_map/all_to_all | solution.py:16
  162.4 0.9 broadcast_in_dim.62
  163.2 4.8 %all-to-all-start.6 = ((bf16[16,16,1024]{2,1,0:T(8,128)(2,1)}), bf16[16,16,1024]{2,1,0:T(8,128)(2,1)S(1)}, u32[]{:S(2)}, u32[]{:S(2)}) async-start(bf16[16,16,1024]{2,1,0:T(8,128)(2,1)} %broadcast_in_dim.62), calls=%async_computation.6 | async-start | bytes 1048576 | tf_op jit(solution)/shard_map/all_to_all | solution.py:16
  168.0 0.5 fusion.1
  169.0 14.0 %all-to-all-done.6 = bf16[16,16,1024]{2,1,0:T(8,128)(2,1)S(1)} async-done(((bf16[16,16,1024]{2,1,0:T(8,128)(2,1)}), bf16[16,16,1024]{2,1,0:T(8,128)(2,1)S(1)}, u32[]{:S(2)}, u32[]{:S(2)}) %all-to-all-start.6) | async-done | bytes 524320 | tf_op jit(solution)/shard_map/all_to_all | solution.py:16
  183.0 0.5 fusion
  184.2 34.1 %all_to_all.46.parts_ref = bf16[16,512,128]{2,1,0:T(8,128)(2,1)} all-to-all(bf16[16,512,128]{2,1,0:T(8,128)(2,1)S(1)} %bitcast.90), channel_id=1, replica_groups=mesh['dp'=16,'lat'=16] {'lat'}, dimensions={0} | all-to-all | bytes 4194304 | tf_op jit(solution)/shard_map/all_to_all | solution.py:16
  218.3 3.1 %gather_sum.1 = bf16[32,64,128]{2,1,0:T(8,128)(2,1)} custom-call(s32[16,8]{1,0:T(8,128)} %slice_clamp_fusion.ids_ref, bf16[16,512,128]{2,1,0:T(8,128)(2,1)} %all_to_all.46.parts_ref), custom_call_target="tpu_custom_call" | custom-call | tf_op jit(solution)/shard_map/gather_sum/pallas_call | solution.py:74
  221.4 6.4 %all-to-all-start.8 = ((bf16[16,128,128]{2,1,0:T(8,128)(2,1)}), bf16[16,128,128]{2,1,0:T(8,128)(2,1)S(1)}, u32[]{:S(2)}, u32[]{:S(2)}) async-start(bf16[16,128,128]{2,1,0:T(8,128)(2,1)} %bitcast.97), calls=%async_computation.8 | async-start | bytes 1048576 | tf_op jit(solution)/shard_map/all_to_all | solution.py:16
  227.8 4.2 %collective-permute-start.1 = (bf16[256,512]{1,0:T(8,128)(2,1)S(1)}, bf16[256,512]{1,0:T(8,128)(2,1)S(1)}, u32[]{:S(2)}, u32[]{:S(2)}) collective-permute-start(bf16[256,512]{1,0:T(8,128)(2,1)S(1)} %subtract_convert_fusion), channel_id=1, source_target_pairs={{0,0},{16,1},{32,2},{48,3},{64,4},{80,5},{96,6},{112,7},{128,8},{1... | collective-permute-start | bytes 786440 | tf_op jit(solution)/shard_map/ppermute | solution.py:134
  232.0 17.6 %collective-permute-done.1 = bf16[256,512]{1,0:T(8,128)(2,1)S(1)} collective-permute-done((bf16[256,512]{1,0:T(8,128)(2,1)S(1)}, bf16[256,512]{1,0:T(8,128)(2,1)S(1)}, u32[]{:S(2)}, u32[]{:S(2)}) %collective-permute-start.1) | collective-permute-done | bytes 262176 | tf_op jit(solution)/shard_map/ppermute | solution.py:134
  249.8 0.4 copy.43
  250.2 1.0 copy.44
  251.2 0.4 copy.42
  251.6 0.8 copy.65
  252.5 0.7 copy.68
  (44 shorter events, 2.4 us)
Async XLA Ops:
  2.6 18.0 %all-to-all-start = ((s32[16,1,128]{2,1,0:T(1,128)}), s32[16,1,128]{2,1,0:T(1,128)S(1)}, u32[]{:S(2)}, u32[]{:S(2)}) async-start(s32[16,1,128]{2,1,0:T(1,128)} %broadcast_in_dim.32), calls=%async_computation | async-start | bytes 16384 | tf_op jit(solution)/shard_map/all_to_all | solution.py:16
  13.2 2.1 copy-start.5
  20.6 16.9 %all-to-all-start.1 = ((bf16[16,136,128]{2,1,0:T(8,128)(2,1)}), bf16[16,136,128]{2,1,0:T(8,128)(2,1)S(1)}, u32[]{:S(2)}, u32[]{:S(2)}) async-start(bf16[16,136,128]{2,1,0:T(8,128)(2,1)} %pad_maximum_fusion.1), calls=%async_computation.1 | async-start | bytes 1114112 | tf_op jit(solution)/shard_map/all_to_all | solution.py:16
  37.5 0.8 copy-start
  41.8 6.7 %copy-start.4 = (bf16[512]{0:T(512)(128)(2,1)S(1)}, bf16[512]{0:T(512)(128)(2,1)}, u32[]{:S(2)}) copy-start(bf16[512]{0:T(512)(128)(2,1)} %param.11) | copy-start | bytes 3076
  41.8 6.7 %copy-start.3 = (bf16[256,512]{1,0:T(8,128)(2,1)S(1)}, bf16[256,512]{1,0:T(8,128)(2,1)}, u32[]{:S(2)}) copy-start(bf16[256,512]{1,0:T(8,128)(2,1)} %param.7) | copy-start | bytes 786436
  41.8 38.7 %all-to-all-start.2 = ((bf16[16,512,128]{2,1,0:T(8,128)(2,1)}), bf16[16,512,128]{2,1,0:T(8,128)(2,1)S(1)}, u32[]{:S(2)}, u32[]{:S(2)}) async-start(bf16[16,512,128]{2,1,0:T(8,128)(2,1)} %pick.1), calls=%async_computation.2 | async-start | bytes 4194304 | tf_op jit(solution)/shard_map/all_to_all | solution.py:16
  48.6 21.5 %collective-permute-start = (bf16[272,512]{1,0:T(8,128)(2,1)S(1)}, bf16[272,512]{1,0:T(8,128)(2,1)S(1)}, u32[]{:S(2)}, u32[]{:S(2)}) collective-permute-start(bf16[272,512]{1,0:T(8,128)(2,1)S(1)} %pad_maximum_fusion.2), channel_id=1, source_target_pairs={{0,0},{1,16},{2,32},{3,48},{4,64},{5,80},{6,96},{7,112},{8,128},{9... | collective-permute-start | bytes 835592 | tf_op jit(solution)/shard_map/ppermute | solution.py:95
  70.1 11.4 %copy-start.1 = (bf16[272,512]{1,0:T(8,128)(2,1)}, bf16[272,512]{1,0:T(8,128)(2,1)S(1)}, u32[]{:S(2)}) copy-start(bf16[272,512]{1,0:T(8,128)(2,1)S(1)} %collective-permute-done) | copy-start | bytes 835588
  81.7 1.0 slice-start
  84.1 41.9 %copy-start.2 = (bf16[272,512]{1,0:T(8,128)(2,1)S(1)}, bf16[272,512]{1,0:T(8,128)(2,1)}, u32[]{:S(2)}) copy-start(bf16[272,512]{1,0:T(8,128)(2,1)} %copy-done.1) | copy-start | bytes 835588
  84.1 36.6 %all-to-all-start.3 = ((f32[16,16,1024]{2,1,0:T(8,128)}), f32[16,16,1024]{2,1,0:T(8,128)S(1)}, u32[]{:S(2)}, u32[]{:S(2)}) async-start(f32[16,16,1024]{2,1,0:T(8,128)} %fusion.13), calls=%async_computation.3 | async-start | bytes 2097152 | tf_op jit(solution)/shard_map/all_to_all | solution.py:16
  121.6 20.0 %all-to-all-start.4 = ((bf16[16,16,1024]{2,1,0:T(8,128)(2,1)}), bf16[16,16,1024]{2,1,0:T(8,128)(2,1)S(1)}, u32[]{:S(2)}, u32[]{:S(2)}) async-start(bf16[16,16,1024]{2,1,0:T(8,128)(2,1)} %broadcast_in_dim.61), calls=%async_computation.4 | async-start | bytes 1048576 | tf_op jit(solution)/shard_map/all_to_all | solution.py:16
  163.2 19.7 %all-to-all-start.6 = ((bf16[16,16,1024]{2,1,0:T(8,128)(2,1)}), bf16[16,16,1024]{2,1,0:T(8,128)(2,1)S(1)}, u32[]{:S(2)}, u32[]{:S(2)}) async-start(bf16[16,16,1024]{2,1,0:T(8,128)(2,1)} %broadcast_in_dim.62), calls=%async_computation.6 | async-start | bytes 1048576 | tf_op jit(solution)/shard_map/all_to_all | solution.py:16
  221.4 28.2 %all-to-all-start.8 = ((bf16[16,128,128]{2,1,0:T(8,128)(2,1)}), bf16[16,128,128]{2,1,0:T(8,128)(2,1)S(1)}, u32[]{:S(2)}, u32[]{:S(2)}) async-start(bf16[16,128,128]{2,1,0:T(8,128)(2,1)} %bitcast.97), calls=%async_computation.8 | async-start | bytes 1048576 | tf_op jit(solution)/shard_map/all_to_all | solution.py:16
  227.8 21.8 %collective-permute-start.1 = (bf16[256,512]{1,0:T(8,128)(2,1)S(1)}, bf16[256,512]{1,0:T(8,128)(2,1)S(1)}, u32[]{:S(2)}, u32[]{:S(2)}) collective-permute-start(bf16[256,512]{1,0:T(8,128)(2,1)S(1)} %subtract_convert_fusion), channel_id=1, source_target_pairs={{0,0},{16,1},{32,2},{48,3},{64,4},{80,5},{96,6},{112,7},{128,8},{1... | collective-permute-start | bytes 786440 | tf_op jit(solution)/shard_map/ppermute | solution.py:134

commit v2 on v1

--- a/solution.py
+++ b/solution.py
@@ -6,6 +6,7 @@
 from jax.experimental import pallas as pl
 from jax.experimental.pallas import tpu as pltpu
 from jax.sharding import PartitionSpec as P
+
 
 BLK = 128
 F32 = jnp.float32
@@ -81,9 +82,16 @@
     )(ids, parts)
 
 
+def spread_rows(parts, groups):
+    weights, width, cols = parts.shape
+    sub = width // groups
+    rows = parts.reshape(weights, groups, sub, cols // BLK, BLK).transpose(1, 0, 3, 2, 4)
+    return rows.reshape(groups, weights * (cols // BLK) * sub, BLK)
+
+
 def local(tokens, enc_weight, enc_bias, dec_weight, dec_bias, block_ids, counts):
     n_dp, n_lat = lax.axis_size("dp"), lax.axis_size("lat")
-    d, t = lax.axis_index("dp"), lax.axis_index("lat")
+    d = lax.axis_index("dp")
     token_count, width = tokens.shape
     owned = enc_weight.shape[1] // BLK
     blocks = owned * n_lat
@@ -91,38 +99,41 @@
     sub = width // n_lat
     flip = [(i * n_lat + j, j * n_dp + i) for i in range(n_dp) for j in range(n_lat)]
 
+    listed = jnp.concatenate([block_ids, counts[:, None]], axis=1).astype(BF16)
+    listed = jnp.pad(listed, ((0, 0), (0, BLK - slots - 1)))
+    listed = lax.ppermute(listed, ("dp", "lat"), flip)
+
     bias_rows = jnp.broadcast_to(dec_bias[None, :], (16, width))
     moved = lax.ppermute(jnp.concatenate([tokens, bias_rows], axis=0), ("dp", "lat"), flip)
     tok, out_bias = moved[:token_count], moved[token_count : token_count + 1]
 
-    listed = jnp.concatenate([block_ids, counts[:, None]], axis=1)
-    listed = jnp.pad(listed, ((0, 0), (0, BLK - slots - 1)))
-    lists = exchange(jnp.broadcast_to(listed[None], (n_dp, 1, BLK)), "dp")[:, 0, :]
-    ids = jnp.clip(lists[:, :slots], 0, blocks - 1)
-    my_list = lax.dynamic_slice_in_dim(lists, t, 1, 0)
-    my_ids = jnp.clip(my_list[0, :slots], 0, blocks - 1)
-    live = jnp.arange(slots) < my_list[0, slots]
-    live_row = jnp.repeat(live, BLK)[None, :]
-
     enc_part = lax.dynamic_slice_in_dim(enc_weight, d * width, width, 0)
     dec_part = lax.dynamic_slice_in_dim(dec_weight, d * width, width, 1).T
-    spread = jnp.stack([enc_part, dec_part]).reshape(2, n_lat, sub, owned, BLK)
-    spread = spread.transpose(1, 0, 3, 2, 4).reshape(n_lat, 2 * owned * sub, BLK)
-    bias_parts = jnp.stack(split3(enc_bias.reshape(owned, BLK))).reshape(3 * owned, BLK)
-    bias_parts = jnp.pad(bias_parts, ((0, 8 - 3 * owned), (0, 0))).astype(BF16)
-    spread = jnp.concatenate([spread, jnp.broadcast_to(bias_parts[None], (n_lat, 8, BLK))], axis=1)
+    spread = spread_rows(jnp.stack([enc_part, dec_part]), n_lat)
+    main = spread.shape[1]
+    extra = [p.reshape(owned, BLK).astype(BF16) for p in split3(enc_bias)] + [listed]
+    extra = jnp.concatenate(extra, axis=0)
+    extra = jnp.pad(extra, ((0, -extra.shape[0] % 8), (0, 0)))
+    spread = jnp.concatenate([spread, jnp.broadcast_to(extra[None], (n_lat,) + extra.shape)], axis=1)
     table = exchange(spread, "lat")
-    all_bias = table[:, 2 * owned * sub :, :].astype(F32)
-    all_bias = all_bias[:, :owned] + all_bias[:, owned : 2 * owned] + all_bias[:, 2 * owned : 3 * owned]
+    extra = table[:, main:].astype(F32)
+    lists = extra[:, 3 * owned].astype(jnp.int32)
+    ids = jnp.clip(lists[:, :slots], 0, blocks - 1)
+    picked = pick(ids, table, sub)
+    picked = exchange(picked, "lat")
+    my_list = listed[0].astype(F32).astype(jnp.int32)
+    live_row = jnp.repeat(jnp.arange(slots) < my_list[slots], BLK)[None, :]
+    all_bias = extra[:, :owned] + extra[:, owned : 2 * owned] + extra[:, 2 * owned : 3 * owned]
+    my_ids = jnp.clip(my_list[:slots], 0, blocks - 1)
     my_bias = all_bias.reshape(blocks, BLK)[my_ids].reshape(1, slots * BLK)
-    picked = exchange(pick(ids, table, sub), "lat")
     picked = picked.reshape(n_lat, 2, slots, sub, BLK).transpose(1, 0, 3, 2, 4)
     picked = picked.reshape(2, width, slots * BLK)
     enc_sel, dec_sel = picked[0], picked[1]
 
     share = token_count // n_dp
-    partial = jnp.dot(tok, enc_sel, preferred_element_type=F32)
-    preact = jnp.sum(exchange(partial.reshape(n_dp, share, slots * BLK), "dp"), axis=0) + my_bias
+    partial = jnp.dot(tok, enc_sel, preferred_element_type=F32).reshape(n_dp, share, slots * BLK)
+    partial = exchange(partial, "dp")
+    preact = jnp.sum(partial, axis=0) + my_bias
     act_share = jnp.where(live_row, jnp.maximum(preact, 0.0), 0.0)
     gate = act_share > 0
     act_share = act_share.astype(BF16)
@@ -131,24 +142,24 @@
 
     recon = lax.dot_general(acts, dec_sel, (((1,), (1,)), ((), ())), preferred_element_type=F32)
     error = (recon + out_bias.astype(F32) - tok.astype(F32)).astype(BF16)
+    back = jnp.dot(error, dec_sel, preferred_element_type=F32).astype(BF16)
+    back = exchange(back.reshape(n_dp, share, slots * BLK), "dp")
     error_out = lax.ppermute(error, ("dp", "lat"), [(b, a) for a, b in flip])
-
-    back = jnp.dot(error, dec_sel, preferred_element_type=F32).astype(BF16)
-    back = jnp.sum(exchange(back.reshape(n_dp, share, slots * BLK), "dp").astype(F32), axis=0)
-    back = jnp.where(gate, back, 0.0).astype(BF16)
+    back = jnp.where(gate, jnp.sum(back.astype(F32), axis=0), 0.0).astype(BF16)
     gated = exchange(jnp.broadcast_to(back[None], (n_dp, share, slots * BLK)), "dp")
     gated = gated.reshape(token_count, slots * BLK)
 
     over_tokens = (((0,), (0,)), ((), ()))
+    scale = 1.0 / math.sqrt(token_count * n_dp)
     dec_grad = lax.dot_general(error, acts, over_tokens, preferred_element_type=F32).astype(BF16)
     enc_grad = lax.dot_general(tok, gated, over_tokens, preferred_element_type=F32).astype(BF16)
-    grads = jnp.stack([enc_grad, dec_grad]).reshape(2, n_lat, sub, slots, BLK)
-    grads = grads.transpose(1, 0, 3, 2, 4).reshape(n_lat, 2 * slots * sub, BLK)
-    summed = gather_sum(ids, exchange(grads, "lat"), blocks)
-    done = exchange(summed.reshape(n_lat, owned * 2 * sub, BLK), "lat")
-    done = done.reshape(n_lat, owned, 2, sub, BLK).astype(F32) * (1.0 / math.sqrt(token_count * n_dp))
-    enc_out = done[:, :, 0].transpose(0, 2, 1, 3).reshape(width, owned * BLK)
-    dec_out = done[:, :, 1].transpose(1, 3, 0, 2).reshape(owned * BLK, width)
+    parts = spread_rows(jnp.stack([enc_grad, dec_grad]), n_lat)
+    parts = exchange(parts, "lat")
+    total = gather_sum(ids, parts, blocks).reshape(n_lat, owned * 2 * sub, BLK)
+    total = exchange(total, "lat")
+    total = total.reshape(n_lat, owned, 2, sub, BLK).astype(F32) * scale
+    enc_out = total[:, :, 0].transpose(0, 2, 1, 3).reshape(width, owned * BLK)
+    dec_out = total[:, :, 1].transpose(1, 3, 0, 2).reshape(owned * BLK, width)
     return error_out, enc_out, dec_out
 
 

time: 258 us -> 254 us (0.984)
  blocking collectives: 53.8 us -> 73.3 us
  waiting for transfers between devices: 115 us -> 97.3 us
  starting transfers between devices: 54.6 us -> 51.6 us
    all_to_all x2 -> x3, blocking collectives: 53.8 us -> 73.3 us  [exchange(): return lax.all_to_all(x, axis, 0, 0, tiled=False)]
    all_to_all x7 -> x5, starting transfers between devices: 48.2 us -> 33 us  [exchange(): return lax.all_to_all(x, axis, 0, 0, tiled=False)]
    all_to_all x7 -> x5, waiting for transfers between devices: 78.1 us -> 63.3 us  [exchange(): return lax.all_to_all(x, axis, 0, 0, tiled=False)]
    ppermute x0 -> x1, starting transfers between devices: none -> 8.11 us  [local(): listed = lax.ppermute(listed, ('dp', 'lat'), flip)]
    ppermute x1, starting transfers between devices: 2.18 us -> 6.3 us  [local(): lax.ppermute(jnp.concatenate([tokens, bias_rows], axis=0), ('dp', 'lat'),...]
    ppermute x1, waiting for transfers between devices: 19.3 us -> 16.5 us  [local(): lax.ppermute(jnp.concatenate([tokens, bias_rows], axis=0), ('dp', 'lat'),...]
  transfers between devices with their start and end apart: 9 -> 8, of which waited for: 8 -> 6; matrix products, arithmetic and copies ran while one was open for 3% -> 2% of each run, Pallas kernels for 0% -> 0%
where the time goes in v2:
time: 254 us; the launch traced here: 249 us
  waiting for transfers between devices  97.3 us (38%)
  blocking collectives  73.3 us (29%)
  starting transfers between devices  51.6 us (20%)
  local copies, waits for them, and re-layouts  12 us (5%)
  Pallas kernels  6.66 us (3%)
  other arithmetic  3.39 us (1%)
  matrix products  3.25 us (1%)
    all_to_all x3, blocking collectives, exchange(): return lax.all_to_all(x, axis, 0, 0, tiled=False)  73.3 us
    all_to_all x5, waiting for transfers between devices, exchange(): return lax.all_to_all(x, axis, 0, 0, tiled=False)  63.3 us
    all_to_all x5, starting transfers between devices, exchange(): return lax.all_to_all(x, axis, 0, 0, tiled=False)  33 us
    ppermute x1, waiting for transfers between devices, local(): error_out = lax.ppermute(error, ('dp', 'lat'), [(b, a) for a, b in flip])  17.5 us
    ppermute x1, waiting for transfers between devices, local(): lax.ppermute(jnp.concatenate([tokens, bias_rows], axis=0), ('dp', 'lat'),...  16.5 us
    ppermute x1, starting transfers between devices, local(): listed = lax.ppermute(listed, ('dp', 'lat'), flip)  8.11 us
    ppermute x1, starting transfers between devices, local(): lax.ppermute(jnp.concatenate([tokens, bias_rows], axis=0), ('dp', 'lat'),...  6.3 us
  transfers between devices with their start and end apart: 8, of which 6 were waited for; matrix products, arithmetic and copies ran while one was open for 2% of the time, Pallas kernels for 0%

profile of v2, /device:TPU:6, one launch (start us, length us, event | category | flops | bytes accessed | tf_op | source)
XLA Modules:
  0.0 249.2 jit_solution(17937656668566293160)
XLA Ops:
  1.3 0.7 convert.8
  2.0 8.1 %collective-permute-start = (bf16[1,128]{1,0:T(2,128)(2,1)S(1)}, bf16[1,128]{1,0:T(2,128)(2,1)S(1)}, u32[]{:S(2)}, u32[]{:S(2)}) collective-permute-start(bf16[1,128]{1,0:T(2,128)(2,1)S(1)} %fusion.17), channel_id=1, source_target_pairs={{0,0},{1,16},{2,32},{3,48},{4,64},{5,80},{6,96},{7,112},{8,128},{9... | collective-permute-start | bytes 776 | tf_op jit(solution)/shard_map/ppermute | solution.py:104
  10.2 1.0 dynamic-slice_bitcast_fusion
  11.4 1.0 constant_dynamic-slice_fusion
  12.4 0.7 maximum_bitcast_fusion
  13.4 19.5 %all_to_all.40.table_ref = bf16[16,136,128]{2,1,0:T(8,128)(2,1)S(1)} all-to-all(bf16[16,136,128]{2,1,0:T(8,128)(2,1)S(1)} %pad_maximum_fusion.1), channel_id=1, replica_groups=mesh['dp'=16,'lat'=16] {'lat'}, dimensions={0} | all-to-all | bytes 1114112 | tf_op jit(solution)/shard_map/all_to_all | solution.py:17
  32.9 0.7 slice_clamp_fusion.ids_ref
  33.7 3.6 %pick.1 = bf16[16,512,128]{2,1,0:T(8,128)(2,1)} custom-call(s32[16,8]{1,0:T(8,128)} %slice_clamp_fusion.ids_ref, bf16[16,136,128]{2,1,0:T(8,128)(2,1)} %copy-done), custom_call_target="tpu_custom_call" | custom-call | tf_op jit(solution)/shard_map/pick/pallas_call | solution.py:45
  37.3 5.7 %all-to-all-start.1 = ((bf16[16,512,128]{2,1,0:T(8,128)(2,1)}), bf16[16,512,128]{2,1,0:T(8,128)(2,1)S(1)}, u32[]{:S(2)}, u32[]{:S(2)}) async-start(bf16[16,512,128]{2,1,0:T(8,128)(2,1)} %pick.1), calls=%async_computation.1 | async-start | bytes 4194304 | tf_op jit(solution)/shard_map/all_to_all | solution.py:17
  43.0 6.3 %collective-permute-start.1 = (bf16[272,512]{1,0:T(8,128)(2,1)S(1)}, bf16[272,512]{1,0:T(8,128)(2,1)S(1)}, u32[]{:S(2)}, u32[]{:S(2)}) collective-permute-start(bf16[272,512]{1,0:T(8,128)(2,1)S(1)} %pad_maximum_fusion.2), channel_id=1, source_target_pairs={{0,0},{1,16},{2,32},{3,48},{4,64},{5,80},{6,96},{7,112},{8,128},{9... | collective-permute-start | bytes 835592 | tf_op jit(solution)/shard_map/ppermute | solution.py:107
  49.3 16.5 %collective-permute-done.1 = bf16[272,512]{1,0:T(8,128)(2,1)S(1)} collective-permute-done((bf16[272,512]{1,0:T(8,128)(2,1)S(1)}, bf16[272,512]{1,0:T(8,128)(2,1)S(1)}, u32[]{:S(2)}, u32[]{:S(2)}) %collective-permute-start.1) | collective-permute-done | bytes 278560 | tf_op jit(solution)/shard_map/ppermute | solution.py:107
  65.8 9.2 %all-to-all-done.1 = bf16[16,512,128]{2,1,0:T(8,128)(2,1)S(1)} async-done(((bf16[16,512,128]{2,1,0:T(8,128)(2,1)}), bf16[16,512,128]{2,1,0:T(8,128)(2,1)S(1)}, u32[]{:S(2)}, u32[]{:S(2)}) %all-to-all-start.1) | async-done | bytes 2097184 | tf_op jit(solution)/shard_map/all_to_all | solution.py:17
  75.0 1.0 copy.83
  76.0 0.1 fusion.22
  76.1 0.5 reshape.211
  76.6 0.4 slice-done
  77.1 1.4 fusion.23
  78.5 11.5 %all-to-all-start.2 = ((f32[16,16,1024]{2,1,0:T(8,128)}), f32[16,16,1024]{2,1,0:T(8,128)S(1)}, u32[]{:S(2)}, u32[]{:S(2)}) async-start(f32[16,16,1024]{2,1,0:T(8,128)} %fusion.23), calls=%async_computation.2 | async-start | bytes 2097152 | tf_op jit(solution)/shard_map/all_to_all | solution.py:17
  90.1 0.6 slice.46
  90.6 0.6 iota_compare_fusion.1
  91.4 0.6 gather_fusion
  92.0 24.5 %all-to-all-done.2 = f32[16,16,1024]{2,1,0:T(8,128)S(1)} async-done(((f32[16,16,1024]{2,1,0:T(8,128)}), f32[16,16,1024]{2,1,0:T(8,128)S(1)}, u32[]{:S(2)}, u32[]{:S(2)}) %all-to-all-start.2) | async-done | bytes 1048608 | tf_op jit(solution)/shard_map/all_to_all | solution.py:17
  116.6 0.9 broadcast_in_dim.51
  117.4 4.7 %all-to-all-start.3 = ((bf16[16,16,1024]{2,1,0:T(8,128)(2,1)}), bf16[16,16,1024]{2,1,0:T(8,128)(2,1)S(1)}, u32[]{:S(2)}, u32[]{:S(2)}) async-start(bf16[16,16,1024]{2,1,0:T(8,128)(2,1)} %broadcast_in_dim.51), calls=%async_computation.3 | async-start | bytes 1048576 | tf_op jit(solution)/shard_map/all_to_all | solution.py:17
  122.2 15.6 %all-to-all-done.3 = bf16[16,16,1024]{2,1,0:T(8,128)(2,1)S(1)} async-done(((bf16[16,16,1024]{2,1,0:T(8,128)(2,1)}), bf16[16,16,1024]{2,1,0:T(8,128)(2,1)S(1)}, u32[]{:S(2)}, u32[]{:S(2)}) %all-to-all-start.3) | async-done | bytes 524320 | tf_op jit(solution)/shard_map/all_to_all | solution.py:17
  137.8 0.5 subtract_convert_fusion
  138.3 0.4 convolution_convert_fusion.2
  138.7 20.2 %all_to_all.41 = bf16[16,16,1024]{2,1,0:T(8,128)(2,1)S(1)} all-to-all(bf16[16,16,1024]{2,1,0:T(8,128)(2,1)S(1)} %bitcast.99), channel_id=1, replica_groups=mesh['dp'=16,'lat'=16] {'dp'}, dimensions={0} | all-to-all | bytes 1048576 | tf_op jit(solution)/shard_map/all_to_all | solution.py:17
  159.0 0.9 broadcast_in_dim.52
  159.9 4.6 %all-to-all-start.5 = ((bf16[16,16,1024]{2,1,0:T(8,128)(2,1)}), bf16[16,16,1024]{2,1,0:T(8,128)(2,1)S(1)}, u32[]{:S(2)}, u32[]{:S(2)}) async-start(bf16[16,16,1024]{2,1,0:T(8,128)(2,1)} %broadcast_in_dim.52), calls=%async_computation.5 | async-start | bytes 1048576 | tf_op jit(solution)/shard_map/all_to_all | solution.py:17
  164.5 0.5 fusion.1
  165.0 0.3 copy.66
  165.2 0.3 copy.59
  165.5 14.0 %all-to-all-done.5 = bf16[16,16,1024]{2,1,0:T(8,128)(2,1)S(1)} async-done(((bf16[16,16,1024]{2,1,0:T(8,128)(2,1)}), bf16[16,16,1024]{2,1,0:T(8,128)(2,1)S(1)}, u32[]{:S(2)}, u32[]{:S(2)}) %all-to-all-start.5) | async-done | bytes 524320 | tf_op jit(solution)/shard_map/all_to_all | solution.py:17
  179.5 0.5 fusion
  180.0 0.3 copy.65
  180.2 0.3 copy.58
  180.5 0.2 pad_maximum_fusion
  180.7 33.6 %all_to_all.42.parts_ref = bf16[16,512,128]{2,1,0:T(8,128)(2,1)} all-to-all(bf16[16,512,128]{2,1,0:T(8,128)(2,1)S(1)} %bitcast.83), channel_id=1, replica_groups=mesh['dp'=16,'lat'=16] {'lat'}, dimensions={0} | all-to-all | bytes 4194304 | tf_op jit(solution)/shard_map/all_to_all | solution.py:17
  214.3 3.1 %gather_sum.1 = bf16[32,64,128]{2,1,0:T(8,128)(2,1)} custom-call(s32[16,8]{1,0:T(8,128)} %slice_clamp_fusion.ids_ref, bf16[16,512,128]{2,1,0:T(8,128)(2,1)} %all_to_all.42.parts_ref), custom_call_target="tpu_custom_call" | custom-call | tf_op jit(solution)/shard_map/gather_sum/pallas_call | solution.py:75
  217.4 6.4 %all-to-all-start.7 = ((bf16[16,128,128]{2,1,0:T(8,128)(2,1)}), bf16[16,128,128]{2,1,0:T(8,128)(2,1)S(1)}, u32[]{:S(2)}, u32[]{:S(2)}) async-start(bf16[16,128,128]{2,1,0:T(8,128)(2,1)} %bitcast.90), calls=%async_computation.7 | async-start | bytes 1048576 | tf_op jit(solution)/shard_map/all_to_all | solution.py:17
  223.8 4.2 %collective-permute-start.2 = (bf16[256,512]{1,0:T(8,128)(2,1)S(1)}, bf16[256,512]{1,0:T(8,128)(2,1)S(1)}, u32[]{:S(2)}, u32[]{:S(2)}) collective-permute-start(bf16[256,512]{1,0:T(8,128)(2,1)S(1)} %subtract_convert_fusion), channel_id=1, source_target_pairs={{0,0},{16,1},{32,2},{48,3},{64,4},{80,5},{96,6},{112,7},{128,8},{1... | collective-permute-start | bytes 786440 | tf_op jit(solution)/shard_map/ppermute | solution.py:147
  228.0 17.5 %collective-permute-done.2 = bf16[256,512]{1,0:T(8,128)(2,1)S(1)} collective-permute-done((bf16[256,512]{1,0:T(8,128)(2,1)S(1)}, bf16[256,512]{1,0:T(8,128)(2,1)S(1)}, u32[]{:S(2)}, u32[]{:S(2)}) %collective-permute-start.2) | collective-permute-done | bytes 262176 | tf_op jit(solution)/shard_map/ppermute | solution.py:147
  245.8 0.4 copy.61
  246.2 1.0 copy.62
  247.2 0.4 copy.60
  247.6 0.8 copy.85
  248.5 0.7 copy.88
  (43 shorter events, 1.2 us)
Async XLA Ops:
  0.6 11.8 %copy-start.5 = (f32[256]{0:T(256)S(1)}, f32[256]{0:T(256)}, u32[]{:S(2)}) copy-start(f32[256]{0:T(256)} %param.9) | copy-start | bytes 3076
  2.0 11.3 %collective-permute-start = (bf16[1,128]{1,0:T(2,128)(2,1)S(1)}, bf16[1,128]{1,0:T(2,128)(2,1)S(1)}, u32[]{:S(2)}, u32[]{:S(2)}) collective-permute-start(bf16[1,128]{1,0:T(2,128)(2,1)S(1)} %fusion.17), channel_id=1, source_target_pairs={{0,0},{1,16},{2,32},{3,48},{4,64},{5,80},{6,96},{7,112},{8,128},{9... | collective-permute-start | bytes 776 | tf_op jit(solution)/shard_map/ppermute | solution.py:104
  32.9 0.8 copy-start
  37.2 5.7 %copy-start.4 = (bf16[512]{0:T(512)(128)(2,1)S(1)}, bf16[512]{0:T(512)(128)(2,1)}, u32[]{:S(2)}) copy-start(bf16[512]{0:T(512)(128)(2,1)} %param.11) | copy-start | bytes 3076
  37.3 5.7 %copy-start.3 = (bf16[256,512]{1,0:T(8,128)(2,1)S(1)}, bf16[256,512]{1,0:T(8,128)(2,1)}, u32[]{:S(2)}) copy-start(bf16[256,512]{1,0:T(8,128)(2,1)} %param.7) | copy-start | bytes 786436
  37.3 37.7 %all-to-all-start.1 = ((bf16[16,512,128]{2,1,0:T(8,128)(2,1)}), bf16[16,512,128]{2,1,0:T(8,128)(2,1)S(1)}, u32[]{:S(2)}, u32[]{:S(2)}) async-start(bf16[16,512,128]{2,1,0:T(8,128)(2,1)} %pick.1), calls=%async_computation.1 | async-start | bytes 4194304 | tf_op jit(solution)/shard_map/all_to_all | solution.py:17
  43.0 22.8 %collective-permute-start.1 = (bf16[272,512]{1,0:T(8,128)(2,1)S(1)}, bf16[272,512]{1,0:T(8,128)(2,1)S(1)}, u32[]{:S(2)}, u32[]{:S(2)}) collective-permute-start(bf16[272,512]{1,0:T(8,128)(2,1)S(1)} %pad_maximum_fusion.2), channel_id=1, source_target_pairs={{0,0},{1,16},{2,32},{3,48},{4,64},{5,80},{6,96},{7,112},{8,128},{9... | collective-permute-start | bytes 835592 | tf_op jit(solution)/shard_map/ppermute | solution.py:107
  65.8 10.2 %copy-start.1 = (bf16[272,512]{1,0:T(8,128)(2,1)}, bf16[272,512]{1,0:T(8,128)(2,1)S(1)}, u32[]{:S(2)}) copy-start(bf16[272,512]{1,0:T(8,128)(2,1)S(1)} %collective-permute-done.1) | copy-start | bytes 835588
  76.1 1.0 slice-start
  78.5 43.7 %copy-start.2 = (bf16[272,512]{1,0:T(8,128)(2,1)S(1)}, bf16[272,512]{1,0:T(8,128)(2,1)}, u32[]{:S(2)}) copy-start(bf16[272,512]{1,0:T(8,128)(2,1)} %copy-done.1) | copy-start | bytes 835588
  78.5 38.0 %all-to-all-start.2 = ((f32[16,16,1024]{2,1,0:T(8,128)}), f32[16,16,1024]{2,1,0:T(8,128)S(1)}, u32[]{:S(2)}, u32[]{:S(2)}) async-start(f32[16,16,1024]{2,1,0:T(8,128)} %fusion.23), calls=%async_computation.2 | async-start | bytes 2097152 | tf_op jit(solution)/shard_map/all_to_all | solution.py:17
  117.4 20.4 %all-to-all-start.3 = ((bf16[16,16,1024]{2,1,0:T(8,128)(2,1)}), bf16[16,16,1024]{2,1,0:T(8,128)(2,1)S(1)}, u32[]{:S(2)}, u32[]{:S(2)}) async-start(bf16[16,16,1024]{2,1,0:T(8,128)(2,1)} %broadcast_in_dim.51), calls=%async_computation.3 | async-start | bytes 1048576 | tf_op jit(solution)/shard_map/all_to_all | solution.py:17
  159.9 19.6 %all-to-all-start.5 = ((bf16[16,16,1024]{2,1,0:T(8,128)(2,1)}), bf16[16,16,1024]{2,1,0:T(8,128)(2,1)S(1)}, u32[]{:S(2)}, u32[]{:S(2)}) async-start(bf16[16,16,1024]{2,1,0:T(8,128)(2,1)} %broadcast_in_dim.52), calls=%async_computation.5 | async-start | bytes 1048576 | tf_op jit(solution)/shard_map/all_to_all | solution.py:17
  217.4 28.2 %all-to-all-start.7 = ((bf16[16,128,128]{2,1,0:T(8,128)(2,1)}), bf16[16,128,128]{2,1,0:T(8,128)(2,1)S(1)}, u32[]{:S(2)}, u32[]{:S(2)}) async-start(bf16[16,128,128]{2,1,0:T(8,128)(2,1)} %bitcast.90), calls=%async_computation.7 | async-start | bytes 1048576 | tf_op jit(solution)/shard_map/all_to_all | solution.py:17
  223.8 21.8 %collective-permute-start.2 = (bf16[256,512]{1,0:T(8,128)(2,1)S(1)}, bf16[256,512]{1,0:T(8,128)(2,1)S(1)}, u32[]{:S(2)}, u32[]{:S(2)}) collective-permute-start(bf16[256,512]{1,0:T(8,128)(2,1)S(1)} %subtract_convert_fusion), channel_id=1, source_target_pairs={{0,0},{16,1},{32,2},{48,3},{64,4},{80,5},{96,6},{112,7},{128,8},{1... | collective-permute-start | bytes 786440 | tf_op jit(solution)/shard_map/ppermute | solution.py:147
